TPU v7x, 32 devices: a whole 2x2x4 slice. The times are simulated.
32 devices in a mesh: groups: 2 (over y), wide: 4 (over z), narrow: 2 (over x), inner: 2 (over core).
Axes of the slice: x: 2, y: 2, z: 4, core: 2. Of those that a mesh axis runs over, the one named last changes fastest.
Arguments:
- tokens: bfloat16 [128, 6144], P(('groups', 'wide'), ('narrow', 'inner')), parts along dimension 0, may hold values from -6 to 6
- cotangent: bfloat16 [128, 6144], P(('groups', 'wide'), ('narrow', 'inner')), parts along dimension 0, may hold values from -3 to 3
- w_gate: bfloat16 [6144, 16384], P(('narrow', 'inner'), 'wide'), may hold values from -0.078125 to 0.078125
- w_up: bfloat16 [6144, 16384], P(('narrow', 'inner'), 'wide'), may hold values from -0.078125 to 0.078125
- w_down: bfloat16 [16384, 6144], P('wide', ('narrow', 'inner')), may hold values from -0.046875 to 0.046875
Outputs:
- output: bfloat16 [128, 6144], P(('groups', 'wide'), ('narrow', 'inner')), parts along dimension 0
- grad_input: bfloat16 [128, 6144], P(('groups', 'wide'), ('narrow', 'inner')), parts along dimension 0
- grad_wgate: bfloat16 [12288, 16384], P(('groups', 'narrow', 'inner'), 'wide'), parts along dimension 0
- grad_wup: bfloat16 [12288, 16384], P(('groups', 'narrow', 'inner'), 'wide'), parts along dimension 0
- grad_wdown: bfloat16 [32768, 6144], P(('groups', 'wide'), ('narrow', 'inner')), parts along dimension 0
There are 2 independent parts, one for each index of `groups`. A program takes and returns all parts, laid end to end along the dimension named above; an argument that names none is the same for every part. Nothing has to cross between parts.
All inputs are finite; a program needn't handle non-finite values.
Results may differ from a plain program's by a relative error of at most 0.012.
Values may be sent and summed in bfloat16 or wider, within the bound.
No kernel may reach another device: no remote copies, remote signals or barrier semaphores. Data moves between devices by JAX's collectives and lax.ppermute only.
A program may use at most 192 MiB of HBM per device.

v0:
```python
import jax
import jax.numpy as jnp
from jax import lax
from jax.sharding import PartitionSpec as P


def contract_last(left, right):
    return lax.dot_general(
        left, right, (((1,), (1,)), ((), ())), preferred_element_type=jnp.float32
    )


def contract_first(left, right):
    return lax.dot_general(
        left, right, (((0,), (0,)), ((), ())), preferred_element_type=jnp.float32
    )


def activate(gate, up):
    return (gate * jax.nn.sigmoid(gate) * up).astype(jnp.bfloat16)


def grad_parts(gate, up, upstream):
    sigmoid_gate = jax.nn.sigmoid(gate)
    grad_gate = (upstream * up * sigmoid_gate * (1.0 + gate * (1.0 - sigmoid_gate))).astype(
        jnp.bfloat16
    )
    grad_up = (upstream * gate * sigmoid_gate).astype(jnp.bfloat16)
    return (grad_gate, grad_up)


def body(tokens, cotangent, w_gate, w_up, w_down):
    gathered = lax.all_gather(tokens, "wide", axis=0, tiled=True)
    gate_part = jnp.dot(gathered, w_gate, preferred_element_type=jnp.float32)
    up_part = jnp.dot(gathered, w_up, preferred_element_type=jnp.float32)
    gate, up = lax.psum((gate_part, up_part), ("narrow", "inner"))
    hidden = activate(gate, up)
    output = lax.psum_scatter(
        jnp.dot(hidden, w_down, preferred_element_type=jnp.float32).astype(jnp.bfloat16),
        "wide",
        scatter_dimension=0,
        tiled=True,
    )
    cot_all = lax.all_gather(cotangent, "wide", axis=0, tiled=True)
    upstream_part = contract_last(cot_all, w_down)
    grad_wdown = contract_first(hidden, cot_all).astype(jnp.bfloat16)
    upstream = lax.psum(upstream_part, ("narrow", "inner"))
    grad_gate, grad_up = grad_parts(gate, up, upstream)
    grad_input = lax.psum_scatter(
        (contract_last(grad_gate, w_gate) + contract_last(grad_up, w_up)).astype(jnp.bfloat16),
        "wide",
        scatter_dimension=0,
        tiled=True,
    )
    grad_wgate = contract_first(gathered, grad_gate).astype(jnp.bfloat16)
    grad_wup = contract_first(gathered, grad_up).astype(jnp.bfloat16)
    return (output, grad_input, grad_wgate, grad_wup, grad_wdown)


def solution(mesh):
    return jax.shard_map(
        body,
        mesh=mesh,
        in_specs=(
            P(("groups", "wide"), ("narrow", "inner")),
            P(("groups", "wide"), ("narrow", "inner")),
            P(("narrow", "inner"), "wide"),
            P(("narrow", "inner"), "wide"),
            P("wide", ("narrow", "inner")),
        ),
        out_specs=(
            P(("groups", "wide"), ("narrow", "inner")),
            P(("groups", "wide"), ("narrow", "inner")),
            P(("groups", "narrow", "inner"), "wide"),
            P(("groups", "narrow", "inner"), "wide"),
            P(("groups", "wide"), ("narrow", "inner")),
        ),
        check_vma=False,
    )
```

profile of v0, /device:TPU:0, one launch (start us, length us, event | category | flops | bytes accessed | tf_op | source)
XLA Modules:
  0.0 206.2 jit_solution(17270711638761119251)
XLA Ops:
  7.2 0.0 all-reduce.3.cloned.1.call-start
  7.2 0.0 copy-start
  7.2 15.8 %all_gather.6 = bf16[64,1536]{1,0:T(8,128)(2,1)S(1)} all-gather(bf16[16,1536]{1,0:T(8,128)(2,1)} %param.5), channel_id=1, replica_groups=mesh['groups'=2,'wide'=4,'narrow'=2,'inner'=2] {'wide'}, dimensions={0}, use_global_device_ids=true | all-gather | bytes 245760 | tf_op jit(solution)/shard_map/all_gather | solution.py:33
  23.0 8.0 %fusion.4 = f32[64,4096]{1,0:T(8,128)} fusion(bf16[64,1536]{1,0:T(8,128)(2,1)S(1)} %all_gather.6, bf16[1536,4096]{1,0:T(8,128)(2,1)} %param.8), kind=kOutput, calls=%fused_computation.13 | convolution fusion | flops 805306368 | bytes 13828096 | tf_op jit(solution)/shard_map/dot_general | solution.py:35
  31.0 0.0 copy-done
  31.0 3.3 %fusion.3 = f32[64,4096]{1,0:T(8,128)} fusion(bf16[64,1536]{1,0:T(8,128)(2,1)S(1)} %all_gather.6, bf16[1536,4096]{1,0:T(8,128)(2,1)S(1)} %copy-done), kind=kOutput, calls=%fused_computation.12 | convolution fusion | flops 805306368 | bytes 13828096 | tf_op jit(solution)/shard_map/dot_general | solution.py:34
  34.3 0.0 copy-done.1
  34.3 14.0 %all_gather.7 = bf16[64,1536]{1,0:T(8,128)(2,1)S(1)} all-gather(bf16[16,1536]{1,0:T(8,128)(2,1)S(1)} %copy-done.1), channel_id=1, replica_groups=mesh['groups'=2,'wide'=4,'narrow'=2,'inner'=2] {'wide'}, dimensions={0}, use_global_device_ids=true | all-gather | bytes 245760 | tf_op jit(solution)/shard_map/all_gather | solution.py:44
  48.3 0.0 slice-done
  48.3 0.0 slice-done.1
  48.3 0.0 slice-done.2
  48.3 4.9 %fusion.5 = f32[64,4096]{1,0:T(8,128)} fusion(bf16[64,1536]{1,0:T(8,128)(2,1)S(1)} %all_gather.7, bf16[4096,1536]{1,0:T(8,128)(2,1)S(1)} %bitcast.23), kind=kOutput, calls=%fused_computation.14 | convolution fusion | flops 805306368 | bytes 13828096 | tf_op jit(solution)/shard_map/dot_general | solution.py:8
  53.2 0.0 all-reduce.3.cloned.1.call-update
  53.2 0.0 reduce-scatter.3.cloned.1.call-start
  53.3 69.9 %all-reduce.3.cloned.1.call-done = (f32[64,4096]{1,0:T(8,128)}, f32[64,4096]{1,0:T(8,128)}, f32[64,4096]{1,0:T(8,128)}) async-done(((f32[64,4096]{1,0:T(8,128)}, f32[64,4096]{1,0:T(8,128)}, f32[64,4096]{1,0:T(8,128)}), (f32[64,4096]{1,0:T(8,128)}, f32[64,4096]{1,0:T(8,128)}, f32[64,4096]{1,0:T(8,128)})) %all-reduce.3.cloned.1.call-update) | async-done | bytes 3145744 | tf_op jit(solution)/shard_map/psum | solution.py:36
  123.2 2.4 %multiply_convert_fusion = (bf16[64,4096]{1,0:T(8,128)(2,1)S(1)}, bf16[64,4096]{1,0:T(8,128)(2,1)S(1)}, bf16[64,4096]{1,0:T(8,128)(2,1)S(1)}) fusion(f32[64,4096]{1,0:T(8,128)} %get-tuple-element.12, f32[64,4096]{1,0:T(8,128)} %get-tuple-element.11, f32[64,4096]{1,0:T(8,128)} %get-tuple-element.10), kind=kLoop, calls=%fused_computation.8 | loop fusion | flops 4194304 | bytes 4718592 | tf_op jit(solution)/shard_map/convert_element_type | solution.py:28
  125.6 0.0 slice-start.3
  125.6 0.0 slice-start.4
  125.6 8.7 %fusion.6 = f32[64,1536]{1,0:T(8,128)S(1)} fusion(bf16[64,4096]{1,0:T(8,128)(2,1)S(1)} %get-tuple-element.14, bf16[1536,4096]{1,0:T(8,128)(2,1)} %param.7), kind=kOutput, calls=%fused_computation.15 | convolution fusion | flops 805306368 | bytes 13500416 | tf_op jit(solution)/shard_map/dot_general | solution.py:8
  134.3 0.0 slice-start.5
  134.3 6.6 %fusion = bf16[1536,4096]{0,1:T(8,128)(2,1)} fusion(bf16[64,4096]{1,0:T(8,128)(2,1)S(1)} %get-tuple-element.14, bf16[64,1536]{1,0:T(8,128)(2,1)S(1)} %all_gather.6), kind=kOutput, calls=%fused_computation.3 | convolution fusion | flops 811597824 | bytes 13303808 | tf_op jit(solution)/shard_map/dot_general | solution.py:14
  140.9 0.0 slice-done.3
  140.9 0.0 slice-done.4
  141.0 3.0 %convolution_convert_fusion.3 = bf16[64,1536]{1,0:T(8,128)(2,1)} fusion(bf16[64,4096]{1,0:T(8,128)(2,1)S(1)} %get-tuple-element.15, bf16[4096,1536]{1,0:T(8,128)(2,1)S(1)} %bitcast.25), kind=kOutput, calls=%fused_computation.7 | convolution fusion | flops 805404672 | bytes 13303808 | tf_op jit(solution)/shard_map/dot_general | solution.py:39
  143.9 0.0 reduce-scatter.3.cloned.1.call-update
  144.0 0.2 reduce-scatter.5.cloned.1.call-start
  144.2 6.4 %fusion.1 = bf16[1536,4096]{0,1:T(8,128)(2,1)} fusion(bf16[64,4096]{1,0:T(8,128)(2,1)S(1)} %get-tuple-element.13, bf16[64,1536]{1,0:T(8,128)(2,1)S(1)} %all_gather.6), kind=kOutput, calls=%fused_computation.4 | convolution fusion | flops 811597824 | bytes 13303808 | tf_op jit(solution)/shard_map/dot_general | solution.py:14
  150.6 9.2 %fusion.2 = bf16[64,1536]{1,0:T(8,128)(2,1)} fusion(f32[64,1536]{1,0:T(8,128)S(1)} %fusion.6, bf16[64,4096]{1,0:T(8,128)(2,1)S(1)} %get-tuple-element.13, bf16[1536,4096]{1,0:T(8,128)(2,1)} %param.8), kind=kOutput, calls=%fused_computation.6 | convolution fusion | flops 805502976 | bytes 13697024 | tf_op jit(solution)/shard_map/dot_general | solution.py:8
  159.8 0.0 reduce-scatter.5.cloned.1.call-update
  159.8 6.6 %convolution_convert_fusion = bf16[4096,1536]{1,0:T(8,128)(2,1)} fusion(bf16[64,4096]{1,0:T(8,128)(2,1)S(1)} %get-tuple-element.15, bf16[64,1536]{1,0:T(8,128)(2,1)S(1)} %all_gather.7), kind=kOutput, calls=%fused_computation | convolution fusion | flops 811597824 | bytes 13303808 | tf_op jit(solution)/shard_map/dot_general | solution.py:14
  166.4 16.6 %copy.10 = bf16[1536,4096]{1,0:T(8,128)(2,1)} copy(bf16[1536,4096]{0,1:T(8,128)(2,1)} %fusion) | data formatting | bytes 25165824
  183.0 16.6 %copy.11 = bf16[1536,4096]{1,0:T(8,128)(2,1)} copy(bf16[1536,4096]{0,1:T(8,128)(2,1)} %fusion.1) | data formatting | bytes 25165824
  (9 shorter events, 0.0 us)
Async XLA Ops:
  7.2 116.0 %all-reduce.3.cloned.1.call-start = ((), (), s32[]{:S(2)}) async-start(), calls=%async_computation.4 | async-start | bytes 6291456 | tf_op jit(solution)/shard_map/psum | solution.py:36
  7.2 23.8 %copy-start = (bf16[1536,4096]{1,0:T(8,128)(2,1)S(1)}, bf16[1536,4096]{1,0:T(8,128)(2,1)}, u32[]{:S(2)}) copy-start(bf16[1536,4096]{1,0:T(8,128)(2,1)} %param.7) | copy-start | bytes 37748740
  23.0 25.3 %slice-start = ((s8[12582912]{0:T(1024)(128)(4,1)}), s8[4194304]{0:T(1024)(128)(4,1)S(1)}, s32[]{:S(2)}) async-start(s8[12582912]{0:T(1024)(128)(4,1)} %bitcast.22), calls=%async_computation.5 | async-start | bytes 8388608
  23.0 25.3 %slice-start.1 = ((s8[12582912]{0:T(1024)(128)(4,1)}), s8[4194304]{0:T(1024)(128)(4,1)S(1)}, s32[]{:S(2)}) async-start(s8[12582912]{0:T(1024)(128)(4,1)} %bitcast.22), calls=%async_computation.6 | async-start | bytes 8388608
  31.0 3.3 %copy-start.1 = (bf16[16,1536]{1,0:T(8,128)(2,1)S(1)}, bf16[16,1536]{1,0:T(8,128)(2,1)}, u32[]{:S(2)}) copy-start(bf16[16,1536]{1,0:T(8,128)(2,1)} %param.6) | copy-start | bytes 147460
  31.0 17.3 %slice-start.2 = ((s8[12582912]{0:T(1024)(128)(4,1)}), s8[4194304]{0:T(1024)(128)(4,1)S(1)}, s32[]{:S(2)}) async-start(s8[12582912]{0:T(1024)(128)(4,1)} %bitcast.22), calls=%async_computation.7 | async-start | bytes 8388608
  53.2 146.4 %reduce-scatter.3.cloned.1.call-start = ((), (), s32[]{:S(2)}) async-start(), calls=%async_computation.2 | async-start | bytes 245760 | tf_op jit(solution)/shard_map/reduce_scatter | solution.py:38
  125.6 15.3 %slice-start.3 = ((s8[12582912]{0:T(1024)(128)(4,1)}), s8[4194304]{0:T(1024)(128)(4,1)S(1)}, s32[]{:S(2)}) async-start(s8[12582912]{0:T(1024)(128)(4,1)} %bitcast.24), calls=%async_computation.8 | async-start | bytes 8388608
  125.6 15.3 %slice-start.4 = ((s8[12582912]{0:T(1024)(128)(4,1)}), s8[4194304]{0:T(1024)(128)(4,1)S(1)}, s32[]{:S(2)}) async-start(s8[12582912]{0:T(1024)(128)(4,1)} %bitcast.24), calls=%async_computation.9 | async-start | bytes 8388608
  134.3 6.6 %slice-start.5 = ((s8[12582912]{0:T(1024)(128)(4,1)}), s8[4194304]{0:T(1024)(128)(4,1)S(1)}, s32[]{:S(2)}) async-start(s8[12582912]{0:T(1024)(128)(4,1)} %bitcast.24), calls=%async_computation.10 | async-start | bytes 8388608
  144.0 55.7 %reduce-scatter.5.cloned.1.call-start = ((), (), s32[]{:S(2)}) async-start(), calls=%async_computation.3 | async-start | bytes 245760 | tf_op jit(solution)/shard_map/reduce_scatter | solution.py:49
Sparse Core Ops, SparseCore 0:
  53.3 69.8 all-reduce.2
  144.1 19.4 reduce-scatter.2
  166.5 17.5 reduce-scatter.4
where the time goes:
time: 207 us; the launch traced here: 206 us
  waiting for transfers between devices  70 us (34%)
  matrix products  56.6 us (27%)
  local copies, waits for them, and re-layouts  33.3 us (16%)
  blocking collectives  29.8 us (14%)
  between operations  13.8 us (7%)
  other arithmetic  2.4 us (1%)
    psum x1, waiting for transfers between devices, body(): gate, up = lax.psum((gate_part, up_part), ('narrow', 'inner'))  69.9 us
    unnamed x18, local copies, waits for them, and re-layouts  33.3 us
    dot_general x3, matrix products, contract_last(): lax.dot_general(left, right, (((1,), (1,)), ((), ())), preferred_element_...  22.7 us
    dot_general x3, matrix products, contract_first(): lax.dot_general(left, right, (((0,), (0,)), ((), ())), preferred_element_...  19.7 us
    all_gather x1, blocking collectives, body(): gathered = lax.all_gather(tokens, 'wide', axis=0, tiled=True)  15.8 us
    all_gather x1, blocking collectives, body(): cot_all = lax.all_gather(cotangent, 'wide', axis=0, tiled=True)  14 us
    dot_general x1, matrix products, body(): up_part = jnp.dot(gathered, w_up, preferred_element_type=jnp.float32)  7.99 us
  transfers between devices with their start and end apart: 3, of which 1 were waited for; matrix products, arithmetic and copies ran while one was open for 27% of the time, Pallas kernels for 0%

commit v1 on v0

--- a/solution.py
+++ b/solution.py
@@ -30,7 +30,12 @@
 
 
 def body(tokens, cotangent, w_gate, w_up, w_down):
-    gathered = lax.all_gather(tokens, "wide", axis=0, tiled=True)
+    ring = [tokens]
+    for hop in range(3):
+        ring.append(lax.ppermute(ring[-1], "wide", [(dev, (dev + 1) % 4) for dev in range(4)]))
+    gathered = jnp.roll(
+        jnp.concatenate(ring[::-1], axis=0), (lax.axis_index("wide") + 1) * ring[0].shape[0], axis=0
+    )
     gate_part = jnp.dot(gathered, w_gate, preferred_element_type=jnp.float32)
     up_part = jnp.dot(gathered, w_up, preferred_element_type=jnp.float32)
     gate, up = lax.psum((gate_part, up_part), ("narrow", "inner"))

time: 207 us -> 199 us (0.961)
  local copies, waits for them, and re-layouts: 33.3 us -> 0.07 us
  waiting for transfers between devices: 70 us -> 97.5 us
  blocking collectives: 29.8 us -> 14.1 us
  matrix products: 56.6 us -> 65.8 us
  starting transfers between devices: 0.3 us -> 5.32 us
    unnamed x18 -> x15, local copies, waits for them, and re-layouts: 33.3 us -> 0.06 us
    reduce_scatter x1, waiting for transfers between devices: 0.01 us -> 20.5 us  [body(): lax.psum_scatter((contract_last(grad_gate, w_gate) + contract_last(grad_u...]
    all_gather x1 -> x0, blocking collectives: 15.8 us -> none  [body(): gathered = lax.all_gather(tokens, 'wide', axis=0, tiled=True)]
    ppermute x0 -> x3, starting transfers between devices: none -> 4.8 us  [body(): lax.ppermute(ring[-1], 'wide', [(dev, (dev + 1) % 4) for dev in range(4)])]
    dot_general x1, matrix products: 3.26 us -> 7.84 us  [body(): gate_part = jnp.dot(gathered, w_gate, preferred_element_type=jnp.float32)]
    dot_general x3, matrix products: 22.7 us -> 27.3 us  [contract_last(): lax.dot_general(left, right, (((1,), (1,)), ((), ())), preferred_element_...]
    ppermute x0 -> x3, waiting for transfers between devices: none -> 4.31 us  [body(): lax.ppermute(ring[-1], 'wide', [(dev, (dev + 1) % 4) for dev in range(4)])]
    reduce_scatter x1, waiting for transfers between devices: 0.01 us -> 3.54 us  [body(): lax.psum_scatter(jnp.dot(hidden, w_down, preferred_element_type=jnp.float...]
  transfers between devices with their start and end apart: 3 -> 6, of which waited for: 1 -> 4; matrix products, arithmetic and copies ran while one was open for 27% -> 13% of each run, Pallas kernels for 0% -> 0%
where the time goes in v1:
time: 199 us
  waiting for transfers between devices  97.5 us (49%)
  matrix products  65.8 us (33%)
  blocking collectives  14.1 us (7%)
  between operations  13.9 us (7%)
  starting transfers between devices  5.32 us (3%)
  other arithmetic  2.4 us (1%)
    psum x1, waiting for transfers between devices, body(): gate, up = lax.psum((gate_part, up_part), ('narrow', 'inner'))  69.1 us
    dot_general x3, matrix products, contract_last(): lax.dot_general(left, right, (((1,), (1,)), ((), ())), preferred_element_...  27.3 us
    reduce_scatter x1, waiting for transfers between devices, body(): lax.psum_scatter((contract_last(grad_gate, w_gate) + contract_last(grad_u...  20.5 us
    dot_general x3, matrix products, contract_first(): lax.dot_general(left, right, (((0,), (0,)), ((), ())), preferred_element_...  19.9 us
    all_gather x1, blocking collectives, body(): cot_all = lax.all_gather(cotangent, 'wide', axis=0, tiled=True)  14.1 us
    dot_general x1, matrix products, body(): up_part = jnp.dot(gathered, w_up, preferred_element_type=jnp.float32)  7.85 us
    dot_general x1, matrix products, body(): gate_part = jnp.dot(gathered, w_gate, preferred_element_type=jnp.float32)  7.84 us
    ppermute x3, starting transfers between devices, body(): lax.ppermute(ring[-1], 'wide', [(dev, (dev + 1) % 4) for dev in range(4)])  4.8 us
  transfers between devices with their start and end apart: 6, of which 4 were waited for; matrix products, arithmetic and copies ran while one was open for 13% of the time, Pallas kernels for 0%

profile of v1, /device:TPU:0, one launch (start us, length us, event | category | flops | bytes accessed | tf_op | source)
XLA Modules:
  0.0 199.0 jit_solution(10423863386936637606)
XLA Ops:
  7.2 0.0 copy-start
  7.2 0.0 all-reduce.3.cloned.1.call-start
  7.2 3.1 %collective-permute-start = (bf16[16,1536]{1,0:T(8,128)(2,1)}, bf16[16,1536]{1,0:T(8,128)(2,1)S(1)}, u32[]{:S(2)}, u32[]{:S(2)}) collective-permute-start(bf16[16,1536]{1,0:T(8,128)(2,1)} %param.5), channel_id=1, source_target_pairs={{0,4},{4,8},{8,12},{12,0},{1,5},{5,9},{9,13},{13,1},{2,6},{6,10},{... | collective-permute-start | bytes 147464 | tf_op jit(solution)/shard_map/ppermute | solution.py:35
  10.3 4.3 %collective-permute-done = bf16[16,1536]{1,0:T(8,128)(2,1)S(1)} collective-permute-done((bf16[16,1536]{1,0:T(8,128)(2,1)}, bf16[16,1536]{1,0:T(8,128)(2,1)S(1)}, u32[]{:S(2)}, u32[]{:S(2)}) %collective-permute-start) | collective-permute-done | bytes 49184 | tf_op jit(solution)/shard_map/ppermute | solution.py:35
  14.6 0.0 collective-permute-start.1
  14.6 14.1 %all_gather.3 = bf16[64,1536]{1,0:T(8,128)(2,1)S(1)} all-gather(bf16[16,1536]{1,0:T(8,128)(2,1)} %param.6), channel_id=1, replica_groups=mesh['groups'=2,'wide'=4,'narrow'=2,'inner'=2] {'wide'}, dimensions={0}, use_global_device_ids=true | all-gather | bytes 245760 | tf_op jit(solution)/shard_map/all_gather | solution.py:49
  28.7 0.0 collective-permute-done.1
  28.7 1.7 collective-permute-start.2
  30.4 9.4 %fusion.11 = f32[64,4096]{1,0:T(8,128)} fusion(bf16[64,1536]{1,0:T(8,128)(2,1)S(1)} %all_gather.3, bf16[4096,1536]{1,0:T(8,128)(2,1)} %param.9), kind=kOutput, calls=%fused_computation.28 | convolution fusion | flops 805306368 | bytes 13828096 | tf_op jit(solution)/shard_map/dot_general | solution.py:8
  39.8 0.0 collective-permute-done.2
  39.9 0.0 copy-done
  40.0 7.8 %fusion.3 = f32[64,4096]{1,0:T(8,128)} fusion(bf16[1536,4096]{1,0:T(8,128)(2,1)} %param.8, bf16[128,1536]{1,0:T(8,128)(2,1)S(1)} %constant_dynamic-update-slice_fusion, s32[]{:T(128)S(6)} %select_n.14), kind=kOutput, calls=%fused_computation.12 | convolution fusion | flops 805306368 | bytes 13828100 | tf_op jit(solution)/shard_map/dot_general | solution.py:40
  47.8 7.8 %fusion.5 = f32[64,4096]{1,0:T(8,128)} fusion(bf16[1536,4096]{1,0:T(8,128)(2,1)} %param.7, bf16[128,1536]{1,0:T(8,128)(2,1)S(1)} %constant_dynamic-update-slice_fusion, s32[]{:T(128)S(6)} %select_n.14), kind=kOutput, calls=%fused_computation.14 | convolution fusion | flops 805306368 | bytes 13828100 | tf_op jit(solution)/shard_map/dot_general | solution.py:39
  55.7 0.0 all-reduce.3.cloned.1.call-update
  55.7 0.2 reduce-scatter.3.cloned.1.call-start
  55.9 69.1 %all-reduce.3.cloned.1.call-done = (f32[64,4096]{1,0:T(8,128)}, f32[64,4096]{1,0:T(8,128)}, f32[64,4096]{1,0:T(8,128)}) async-done(((f32[64,4096]{1,0:T(8,128)}, f32[64,4096]{1,0:T(8,128)}, f32[64,4096]{1,0:T(8,128)}), (f32[64,4096]{1,0:T(8,128)}, f32[64,4096]{1,0:T(8,128)}, f32[64,4096]{1,0:T(8,128)})) %all-reduce.3.cloned.1.call-update) | async-done | bytes 3145744 | tf_op jit(solution)/shard_map/psum | solution.py:41
  125.0 2.4 %multiply_convert_fusion = (bf16[64,4096]{1,0:T(8,128)(2,1)S(1)}, bf16[64,4096]{1,0:T(8,128)(2,1)S(1)}, bf16[64,4096]{1,0:T(8,128)(2,1)S(1)}) fusion(f32[64,4096]{1,0:T(8,128)} %get-tuple-element.7, f32[64,4096]{1,0:T(8,128)} %get-tuple-element.6, f32[64,4096]{1,0:T(8,128)} %get-tuple-element.5), kind=kLoop, calls=%fused_computation.6 | loop fusion | flops 4194304 | bytes 4718592 | tf_op jit(solution)/shard_map/convert_element_type | solution.py:28
  127.4 0.0 slice-start
  127.4 0.0 slice-start.1
  127.4 8.7 %fusion.12 = f32[64,1536]{1,0:T(8,128)S(1)} fusion(bf16[64,4096]{1,0:T(8,128)(2,1)S(1)} %get-tuple-element.9, bf16[1536,4096]{1,0:T(8,128)(2,1)} %param.7), kind=kOutput, calls=%fused_computation.29 | convolution fusion | flops 805306368 | bytes 13500416 | tf_op jit(solution)/shard_map/dot_general | solution.py:8
  136.1 0.0 slice-start.2
  136.1 6.6 %convolution_convert_fusion.2 = bf16[1536,4096]{1,0:T(8,128)(2,1)} fusion(bf16[64,4096]{1,0:T(8,128)(2,1)S(1)} %get-tuple-element.9, bf16[128,1536]{1,0:T(8,128)(2,1)S(1)} %constant_dynamic-update-slice_fusion, s32[]{:T(128)S(6)} %select_n.14), kind=kOutput, calls=%fused_computation.2 | convolution fusion | flops 811597824 | bytes 13303812 | tf_op jit(solution)/shard_map/dot_general | solution.py:14
  142.7 0.0 slice-done
  142.8 3.0 %convolution_convert_fusion.3 = bf16[64,1536]{1,0:T(8,128)(2,1)} fusion(bf16[64,4096]{1,0:T(8,128)(2,1)S(1)} %get-tuple-element.10, bf16[4096,1536]{1,0:T(8,128)(2,1)S(1)} %bitcast.15), kind=kOutput, calls=%fused_computation.5 | convolution fusion | flops 805404672 | bytes 13303808 | tf_op jit(solution)/shard_map/dot_general | solution.py:44
  145.7 6.6 %convolution_convert_fusion = bf16[4096,1536]{1,0:T(8,128)(2,1)} fusion(bf16[64,4096]{1,0:T(8,128)(2,1)S(1)} %get-tuple-element.10, bf16[64,1536]{1,0:T(8,128)(2,1)S(1)} %all_gather.3), kind=kOutput, calls=%fused_computation | convolution fusion | flops 811597824 | bytes 13303808 | tf_op jit(solution)/shard_map/dot_general | solution.py:14
  152.3 0.0 reduce-scatter.3.cloned.1.call-update
  152.3 0.3 reduce-scatter.5.cloned.1.call-start
  152.6 9.2 %fusion = bf16[64,1536]{1,0:T(8,128)(2,1)} fusion(f32[64,1536]{1,0:T(8,128)S(1)} %fusion.12, bf16[64,4096]{1,0:T(8,128)(2,1)S(1)} %get-tuple-element.8, bf16[1536,4096]{1,0:T(8,128)(2,1)} %param.8), kind=kOutput, calls=%fused_computation.4 | convolution fusion | flops 805502976 | bytes 13697024 | tf_op jit(solution)/shard_map/dot_general | solution.py:8
  161.8 0.0 reduce-scatter.5.cloned.1.call-update
  161.8 6.6 %convolution_convert_fusion.1 = bf16[1536,4096]{1,0:T(8,128)(2,1)} fusion(bf16[64,4096]{1,0:T(8,128)(2,1)S(1)} %get-tuple-element.8, bf16[128,1536]{1,0:T(8,128)(2,1)S(1)} %constant_dynamic-update-slice_fusion, s32[]{:T(128)S(6)} %select_n.14), kind=kOutput, calls=%fused_computation.1 | convolution fusion | flops 811597824 | bytes 13303812 | tf_op jit(solution)/shard_map/dot_general | solution.py:14
  168.4 3.5 %reduce-scatter.3.cloned.1.call-done = bf16[16,1536]{1,0:T(8,128)(2,1)} async-done(((bf16[64,1536]{1,0:T(8,128)(2,1)}), bf16[16,1536]{1,0:T(8,128)(2,1)}) %reduce-scatter.3.cloned.1.call-update) | async-done | bytes 49168 | tf_op jit(solution)/shard_map/reduce_scatter | solution.py:43
  172.0 20.5 %reduce-scatter.5.cloned.1.call-done = bf16[16,1536]{1,0:T(8,128)(2,1)} async-done(((bf16[64,1536]{1,0:T(8,128)(2,1)}), bf16[16,1536]{1,0:T(8,128)(2,1)}) %reduce-scatter.5.cloned.1.call-update) | async-done | bytes 49168 | tf_op jit(solution)/shard_map/reduce_scatter | solution.py:54
  (11 shorter events, 0.0 us)
Async XLA Ops:
  7.2 32.7 %copy-start = (bf16[16,1536]{1,0:T(8,128)(2,1)S(1)}, bf16[16,1536]{1,0:T(8,128)(2,1)}, u32[]{:S(2)}) copy-start(bf16[16,1536]{1,0:T(8,128)(2,1)} %param.5) | copy-start | bytes 147460
  7.2 117.8 %all-reduce.3.cloned.1.call-start = ((), (), s32[]{:S(2)}) async-start(), calls=%async_computation.4 | async-start | bytes 6291456 | tf_op jit(solution)/shard_map/psum | solution.py:41
  7.2 7.4 %collective-permute-start = (bf16[16,1536]{1,0:T(8,128)(2,1)}, bf16[16,1536]{1,0:T(8,128)(2,1)S(1)}, u32[]{:S(2)}, u32[]{:S(2)}) collective-permute-start(bf16[16,1536]{1,0:T(8,128)(2,1)} %param.5), channel_id=1, source_target_pairs={{0,4},{4,8},{8,12},{12,0},{1,5},{5,9},{9,13},{13,1},{2,6},{6,10},{... | collective-permute-start | bytes 147464 | tf_op jit(solution)/shard_map/ppermute | solution.py:35
  14.6 14.1 %collective-permute-start.1 = (bf16[16,1536]{1,0:T(8,128)(2,1)S(1)}, bf16[16,1536]{1,0:T(8,128)(2,1)S(1)}, u32[]{:S(2)}, u32[]{:S(2)}) collective-permute-start(bf16[16,1536]{1,0:T(8,128)(2,1)S(1)} %collective-permute-done), channel_id=1, source_target_pairs={{0,4},{4,8},{8,12},{12,0},{1,5},{5,9},{9,13},{13,1},{2,6},{6,10},{... | collective-permute-start | bytes 147464 | tf_op jit(solution)/shard_map/ppermute | solution.py:35
  28.7 11.1 %collective-permute-start.2 = (bf16[16,1536]{1,0:T(8,128)(2,1)S(1)}, bf16[16,1536]{1,0:T(8,128)(2,1)S(1)}, u32[]{:S(2)}, u32[]{:S(2)}) collective-permute-start(bf16[16,1536]{1,0:T(8,128)(2,1)S(1)} %collective-permute-done.1), channel_id=1, source_target_pairs={{0,4},{4,8},{8,12},{12,0},{1,5},{5,9},{9,13},{13,1},{2,6},{6,10},{... | collective-permute-start | bytes 147464 | tf_op jit(solution)/shard_map/ppermute | solution.py:35
  55.7 116.3 %reduce-scatter.3.cloned.1.call-start = ((), (), s32[]{:S(2)}) async-start(), calls=%async_computation.2 | async-start | bytes 245760 | tf_op jit(solution)/shard_map/reduce_scatter | solution.py:43
  127.4 15.3 %slice-start = ((s8[12582912]{0:T(1024)(128)(4,1)}), s8[4194304]{0:T(1024)(128)(4,1)S(1)}, s32[]{:S(2)}) async-start(s8[12582912]{0:T(1024)(128)(4,1)} %bitcast.14), calls=%async_computation.5 | async-start | bytes 8388608
  127.4 15.3 %slice-start.1 = ((s8[12582912]{0:T(1024)(128)(4,1)}), s8[4194304]{0:T(1024)(128)(4,1)S(1)}, s32[]{:S(2)}) async-start(s8[12582912]{0:T(1024)(128)(4,1)} %bitcast.14), calls=%async_computation.6 | async-start | bytes 8388608
  136.1 6.7 %slice-start.2 = ((s8[12582912]{0:T(1024)(128)(4,1)}), s8[4194304]{0:T(1024)(128)(4,1)S(1)}, s32[]{:S(2)}) async-start(s8[12582912]{0:T(1024)(128)(4,1)} %bitcast.14), calls=%async_computation.7 | async-start | bytes 8388608
  152.3 40.2 %reduce-scatter.5.cloned.1.call-start = ((), (), s32[]{:S(2)}) async-start(), calls=%async_computation.3 | async-start | bytes 245760 | tf_op jit(solution)/shard_map/reduce_scatter | solution.py:54
Sparse Core Ops, SparseCore 0:
  55.8 69.1 all-reduce.2
  152.5 19.4 reduce-scatter.2
  174.9 17.5 reduce-scatter.4
